TPU v7x, 32 devices: a whole 2x2x4 slice. The times are simulated.
32 devices in a mesh: replica: 2 (over y), shard: 2 (over x), tensor: 8 (over z, core).
Axes of the slice: x: 2, y: 2, z: 4, core: 2. Of those that a mesh axis runs over, the one named last changes fastest.
Arguments:
- layer_input: bfloat16 [32768, 1024], P(('replica', 'shard', 'tensor')), may hold values from -6 to 6
- segment_ids: int32 [32, 1024], P(('replica', 'shard')), may hold values from 0 to 3, as said below
- qkv_weight: bfloat16 [3, 1024, 1024], P(None, 'shard', 'tensor'), may hold values from -0.1875 to 0.1875
- qkv_bias: float32 [2, 1024], P(None, 'tensor'), may hold values from -1.2 to 1.2
- out_weight: bfloat16 [1024, 1024], P('tensor', 'shard'), may hold values from -1.5 to 1.5
- out_bias: float32 [1024], replicated, may hold values from -3 to 3
- norm1_gain: float32 [1024], replicated, may hold values from 0.5 to 1.5
- norm1_bias: float32 [1024], replicated, may hold values from -3 to 3
- up_weight: bfloat16 [1024, 4096], P('shard', 'tensor'), may hold values from -0.1875 to 0.1875
- up_bias: float32 [4096], P('tensor'), may hold values from -3 to 3
- down_weight: bfloat16 [4096, 1024], P('tensor', 'shard'), may hold values from -0.09375 to 0.09375
- down_bias: float32 [1024], replicated, may hold values from -3 to 3
- norm2_gain: float32 [1024], replicated, may hold values from 0.5 to 1.5
- norm2_bias: float32 [1024], replicated, may hold values from -3 to 3
- output_grad: bfloat16 [32768, 1024], P(('replica', 'shard', 'tensor')), may hold values from -6 to 6
Outputs:
- activations: bfloat16 [32768, 1024], P(('replica', 'shard', 'tensor'))
- input_grad: float32 [32768, 1024], P(('replica', 'shard', 'tensor'))
- qkv_weight_grad: float32 [3, 1024, 1024], P(None, 'shard', 'tensor')
- qkv_bias_grad: float32 [2, 1024], P(None, 'tensor')
- out_weight_grad: float32 [1024, 1024], P('tensor', 'shard')
- out_bias_grad: float32 [1024], replicated
- norm1_gain_grad: float32 [1024], replicated
- norm1_bias_grad: float32 [1024], replicated
- up_weight_grad: float32 [1024, 4096], P('shard', 'tensor')
- up_bias_grad: float32 [4096], P('tensor')
- down_weight_grad: float32 [4096, 1024], P('tensor', 'shard')
- down_bias_grad: float32 [1024], replicated
- norm2_gain_grad: float32 [1024], replicated
- norm2_bias_grad: float32 [1024], replicated
Inputs may be any that keep to these rules, and one draw needn't show every extreme that they name: `segment_ids`: within each sequence the ids never fall and every id from 0 to 3 occurs; each document holds 128 to 512 tokens, and one in each sequence holds exactly 512.
All inputs are finite; a program needn't handle non-finite values.
Results may differ from a plain program's by a relative error of at most 0.02.
Values may be sent and summed in bfloat16 or wider, within the bound.
No kernel may reach another device: no remote copies, remote signals or barrier semaphores. Data moves between devices by JAX's collectives and lax.ppermute only.
A program may use at most 256 MiB of HBM per device.

v0:
```python
import math
import jax
import jax.numpy as jnp
from jax import lax
from jax.sharding import PartitionSpec as P

HEAD_DIM = 64
LEN = 1024
EPSILON = 1e-05
NEG_FILL = -1e30
CONTRACT_ROWS = (((0,), (0,)), ((), ()))
CONTRACT_COLS = (((1,), (1,)), ((), ()))


def layer_weights(qkv_weight, out_weight, up_weight, down_weight):
    return (
        lax.all_gather(qkv_weight, "shard", axis=1, tiled=True),
        lax.all_gather(out_weight, "shard", axis=1, tiled=True),
        lax.all_gather(up_weight, "shard", axis=0, tiled=True),
        lax.all_gather(down_weight, "shard", axis=1, tiled=True),
    )


def input_rows(layer_input):
    return lax.all_gather(layer_input, "tensor", axis=0, tiled=True)


def middle_rows(hidden_low):
    return lax.all_gather(hidden_low, "tensor", axis=0, tiled=True)


def normalize(residual, gain_vec, shift_vec):
    center = residual - jnp.mean(residual, axis=-1, keepdims=True)
    spread = lax.rsqrt(jnp.mean(center * center, axis=-1, keepdims=True) + EPSILON)
    normed = center * spread
    return (normed * gain_vec + shift_vec, normed, spread)


def norm_back(incoming, normed, spread, gain_vec):
    scaled = incoming * gain_vec
    back_grad = spread * (
        scaled
        - jnp.mean(scaled, axis=-1, keepdims=True)
        - normed * jnp.mean(scaled * normed, axis=-1, keepdims=True)
    )
    return (back_grad, jnp.sum(incoming * normed, axis=0), jnp.sum(incoming, axis=0))


def masked_scores(queries, key_rows, segments):
    scores = jnp.einsum(
        "qhd,khd->hqk", queries, key_rows, preferred_element_type=jnp.float32
    ) * HEAD_DIM ** (-0.5)
    same_doc = segments[:, None] == segments[None, :]
    return jnp.where(same_doc[None], scores, NEG_FILL)


def attend(block_item):
    queries, key_rows, value_rows, segments = block_item
    scores = masked_scores(queries, key_rows, segments)
    row_max = jnp.max(scores, axis=-1, keepdims=True)
    raw_weights = jnp.exp(scores - row_max)
    row_total = jnp.sum(raw_weights, axis=-1, keepdims=True)
    attn_probs = raw_weights / row_total
    log_total = row_max + jnp.log(row_total)
    mixed_heads = jnp.einsum(
        "hqk,khd->qhd",
        attn_probs.astype(jnp.bfloat16),
        value_rows,
        preferred_element_type=jnp.float32,
    )
    return (mixed_heads.astype(jnp.bfloat16), log_total)


def attend_back(block_item):
    queries, key_rows, value_rows, segments, log_total, mixed_grad = block_item
    scores = masked_scores(queries, key_rows, segments)
    attn_probs = jnp.exp(scores - log_total)
    prob_grad = jnp.einsum(
        "qhd,khd->hqk", mixed_grad, value_rows, preferred_element_type=jnp.float32
    )
    value_grad = jnp.einsum(
        "hqk,qhd->khd",
        attn_probs.astype(jnp.bfloat16),
        mixed_grad,
        preferred_element_type=jnp.float32,
    )
    inner_sum = jnp.sum(attn_probs * prob_grad, axis=-1, keepdims=True)
    score_low = (attn_probs * (prob_grad - inner_sum)).astype(jnp.bfloat16)
    query_grad = jnp.einsum(
        "hqk,khd->qhd", score_low, key_rows, preferred_element_type=jnp.float32
    ) * HEAD_DIM ** (-0.5)
    key_grad = jnp.einsum(
        "hqk,qhd->khd", score_low, queries, preferred_element_type=jnp.float32
    ) * HEAD_DIM ** (-0.5)
    return (query_grad, key_grad, value_grad)


def body(
    layer_input,
    segment_ids,
    qkv_weight,
    qkv_bias,
    out_weight,
    out_bias,
    norm1_gain,
    norm1_bias,
    up_weight,
    up_bias,
    down_weight,
    down_bias,
    norm2_gain,
    norm2_bias,
    output_grad,
):
    rows_input = input_rows(layer_input)
    group_rows = rows_input.shape[0]
    seq_count = group_rows // LEN
    w_qkv, w_out, w_up, w_down = layer_weights(qkv_weight, out_weight, up_weight, down_weight)
    width = w_qkv.shape[2]
    heads_here = width // HEAD_DIM
    hidden_here = w_up.shape[1]

    def split_heads(rows_array):
        return rows_array.reshape(seq_count, LEN, heads_here, HEAD_DIM)

    projected = jnp.einsum("td,jdc->jtc", rows_input, w_qkv, preferred_element_type=jnp.float32)
    queries = (projected[0] + qkv_bias[0]).astype(jnp.bfloat16)
    key_rows = projected[1].astype(jnp.bfloat16)
    value_rows = (projected[2] + qkv_bias[1]).astype(jnp.bfloat16)
    mixed, log_total = lax.map(
        attend, (split_heads(queries), split_heads(key_rows), split_heads(value_rows), segment_ids)
    )
    mixed_rows = mixed.reshape(group_rows, width)
    row_block = mixed_rows
    attn_local = lax.psum_scatter(
        jnp.dot(row_block, w_out, preferred_element_type=jnp.float32).astype(jnp.bfloat16),
        "tensor",
        scatter_dimension=0,
        tiled=True,
    ).astype(jnp.float32)
    residual_one = layer_input.astype(jnp.float32) + attn_local + out_bias
    hidden_one, normed_one, spread_one = normalize(residual_one, norm1_gain, norm1_bias)
    hidden_low = hidden_one.astype(jnp.bfloat16)
    rows_middle = middle_rows(hidden_low)
    pre_act = jnp.dot(rows_middle, w_up, preferred_element_type=jnp.float32) + up_bias
    activ = jax.nn.gelu(pre_act, approximate=False).astype(jnp.bfloat16)
    row_block = activ
    mlp_local = lax.psum_scatter(
        jnp.dot(row_block, w_down, preferred_element_type=jnp.float32).astype(jnp.bfloat16),
        "tensor",
        scatter_dimension=0,
        tiled=True,
    ).astype(jnp.float32)
    residual_two = hidden_one + mlp_local + down_bias
    final_out, normed_two, spread_two = normalize(residual_two, norm2_gain, norm2_bias)
    resid_two_grad, gain_two_grad, shift_two_grad = norm_back(
        output_grad.astype(jnp.float32), normed_two, spread_two, norm2_gain
    )
    down_bias_part = jnp.sum(resid_two_grad, axis=0)
    branch_grad = resid_two_grad.astype(jnp.bfloat16)
    rows_branch = lax.all_gather(branch_grad, "tensor", axis=0, tiled=True)
    w_qkv, w_out, w_up, w_down = layer_weights(qkv_weight, out_weight, up_weight, down_weight)
    down_grad = lax.dot_general(
        activ, rows_branch, CONTRACT_ROWS, preferred_element_type=jnp.float32
    )
    activ_grad = lax.dot_general(
        rows_branch, w_down, CONTRACT_COLS, preferred_element_type=jnp.float32
    )
    normal_cdf = 0.5 * (1.0 + lax.erf(pre_act * (1.0 / math.sqrt(2.0))))
    normal_pdf = jnp.exp(-0.5 * pre_act * pre_act) * (1.0 / math.sqrt(2.0 * math.pi))
    pre_grad = activ_grad * (normal_cdf + pre_act * normal_pdf)
    up_bias_part = jnp.sum(pre_grad, axis=0)
    pre_low = pre_grad.astype(jnp.bfloat16)
    up_grad = lax.dot_general(
        rows_middle, pre_low, CONTRACT_ROWS, preferred_element_type=jnp.float32
    )
    row_block = pre_low
    back_middle = lax.psum_scatter(
        lax.dot_general(row_block, w_up, CONTRACT_COLS, preferred_element_type=jnp.float32),
        "tensor",
        scatter_dimension=0,
        tiled=True,
    )
    resid_one_grad, gain_one_grad, shift_one_grad = norm_back(
        resid_two_grad + back_middle, normed_one, spread_one, norm1_gain
    )
    out_bias_part = jnp.sum(resid_one_grad, axis=0)
    attn_grad = resid_one_grad.astype(jnp.bfloat16)
    rows_attn = lax.all_gather(attn_grad, "tensor", axis=0, tiled=True)
    out_grad_part = lax.dot_general(
        mixed_rows, rows_attn, CONTRACT_ROWS, preferred_element_type=jnp.float32
    )
    mixed_grad = lax.dot_general(
        rows_attn, w_out, CONTRACT_COLS, preferred_element_type=jnp.float32
    ).astype(jnp.bfloat16)
    query_grad, key_grad, value_grad = lax.map(
        attend_back,
        (
            split_heads(queries),
            split_heads(key_rows),
            split_heads(value_rows),
            segment_ids,
            log_total,
            split_heads(mixed_grad),
        ),
    )
    query_grad = query_grad.reshape(group_rows, width)
    key_grad = key_grad.reshape(group_rows, width)
    value_grad = value_grad.reshape(group_rows, width)
    bias_part = jnp.stack([jnp.sum(query_grad, axis=0), jnp.sum(value_grad, axis=0)])
    proj_low = jnp.stack([query_grad, key_grad, value_grad]).astype(jnp.bfloat16)
    qkv_grad = jnp.einsum("td,jtc->jdc", rows_input, proj_low, preferred_element_type=jnp.float32)
    row_block = proj_low
    back_input = lax.psum_scatter(
        jnp.einsum("jtc,jdc->td", row_block, w_qkv, preferred_element_type=jnp.float32).astype(
            jnp.bfloat16
        ),
        "tensor",
        scatter_dimension=0,
        tiled=True,
    ).astype(jnp.float32)
    input_grad = resid_one_grad + back_input
    qkv_owned, out_owned, up_owned, down_owned = (
        lax.psum_scatter(
            qkv_grad.astype(jnp.bfloat16), "shard", scatter_dimension=1, tiled=True
        ).astype(jnp.float32),
        lax.psum_scatter(
            out_grad_part.astype(jnp.bfloat16), "shard", scatter_dimension=1, tiled=True
        ).astype(jnp.float32),
        lax.psum_scatter(
            up_grad.astype(jnp.bfloat16), "shard", scatter_dimension=0, tiled=True
        ).astype(jnp.float32),
        lax.psum_scatter(
            down_grad.astype(jnp.bfloat16), "shard", scatter_dimension=1, tiled=True
        ).astype(jnp.float32),
    )
    qkv_owned, out_owned, up_owned, down_owned = (
        lax.psum(qkv_owned.astype(jnp.bfloat16), "replica").astype(jnp.float32),
        lax.psum(out_owned.astype(jnp.bfloat16), "replica").astype(jnp.float32),
        lax.psum(up_owned.astype(jnp.bfloat16), "replica").astype(jnp.float32),
        lax.psum(down_owned.astype(jnp.bfloat16), "replica").astype(jnp.float32),
    )
    tensor_index = lax.axis_index("tensor")
    tensor_count = lax.axis_size("tensor")
    bias_full = lax.dynamic_update_slice(
        jnp.zeros((2, width * tensor_count), jnp.float32),
        bias_part,
        (jnp.int32(0), tensor_index * width),
    )
    up_full = lax.dynamic_update_slice_in_dim(
        jnp.zeros((hidden_here * tensor_count,), jnp.float32),
        up_bias_part,
        tensor_index * hidden_here,
        0,
    )
    summed = lax.psum(
        (
            bias_full,
            up_full,
            out_bias_part,
            gain_one_grad,
            shift_one_grad,
            down_bias_part,
            gain_two_grad,
            shift_two_grad,
        ),
        ("replica", "shard", "tensor"),
    )
    qkv_bias_grad = lax.dynamic_slice_in_dim(summed[0], tensor_index * width, width, 1)
    up_bias_grad = lax.dynamic_slice_in_dim(summed[1], tensor_index * hidden_here, hidden_here, 0)
    return (
        final_out.astype(jnp.bfloat16),
        input_grad,
        qkv_owned,
        qkv_bias_grad,
        out_owned,
        summed[2],
        summed[3],
        summed[4],
        up_owned,
        up_bias_grad,
        down_owned,
        summed[5],
        summed[6],
        summed[7],
    )


def solution(mesh):
    placed = (
        P(("replica", "shard", "tensor"), None),
        P(("replica", "shard"), None),
        P(None, "shard", "tensor"),
        P(None, "tensor"),
        P("tensor", "shard"),
        P(),
        P(),
        P(),
        P("shard", "tensor"),
        P("tensor"),
        P("tensor", "shard"),
        P(),
        P(),
        P(),
        P(("replica", "shard", "tensor"), None),
    )
    return jax.shard_map(
        body,
        mesh=mesh,
        in_specs=placed,
        out_specs=(
            P(("replica", "shard", "tensor"), None),
            P(("replica", "shard", "tensor"), None),
            P(None, "shard", "tensor"),
            P(None, "tensor"),
            P("tensor", "shard"),
            P(),
            P(),
            P(),
            P("shard", "tensor"),
            P("tensor"),
            P("tensor", "shard"),
            P(),
            P(),
            P(),
        ),
        check_vma=False,
    )
```

profile of v0, /device:TPU:0, one launch (start us, length us, event | category | flops | bytes accessed | tf_op | source)
XLA Modules:
  0.0 2068.1 jit_solution(11723061719145368283)
XLA Ops:
  10.9 7.4 all_gather.30
  18.3 10.9 all_gather.28
  29.3 135.0 %all-gather.7.cloned.1.call-done = bf16[8192,1024]{1,0:T(8,128)(2,1)} async-done(((bf16[1024,1024]{1,0:T(8,128)(2,1)}), bf16[8192,1024]{1,0:T(8,128)(2,1)}) %all-gather.7.cloned.1.call-update) | async-done | bytes 16777232 | tf_op jit(solution)/shard_map/all_gather | solution.py:25
  164.3 13.2 fusion.73
  201.2 90.2 %while.26 = (s32[]{:T(128)}, bf16[8,1024,2,64]{1,3,2,0:T(8,128)(2,1)}, f32[8,2,1024,1]{2,1,3,0:T(2,128)}, bf16[8,1024,2,64]{1,3,2,0:T(8,128)(2,1)}, s32[8,1024]{...) while((s32[]{:T(128)}, ...), condition=%wide.region_3.4_spmd, body=%wide.region_0.3_spmd.sunk | while | flops 563214336 | bytes 30488676 | solution.py:130
  296.4 8.3 convolution_convert_fusion
  305.3 165.9 %reduce-scatter.9.cloned.1.call-done = bf16[1024,1024]{1,0:T(8,128)(2,1)} async-done(((bf16[8192,1024]{1,0:T(8,128)(2,1)}), bf16[1024,1024]{1,0:T(8,128)(2,1)}) %reduce-scatter.9.cloned.1.call-update) | async-done | bytes 2097168 | tf_op jit(solution)/shard_map/reduce_scatter | solution.py:135
  478.0 148.9 %all-gather.9.cloned.1.call-done = bf16[8192,1024]{1,0:T(8,128)(2,1)} async-done(((bf16[1024,1024]{1,0:T(8,128)(2,1)}), bf16[8192,1024]{1,0:T(8,128)(2,1)}) %all-gather.9.cloned.1.call-update) | async-done | bytes 16777232 | tf_op jit(solution)/shard_map/all_gather | solution.py:29
  626.8 47.4 %fusion.56 = (bf16[8192,512]{1,0:T(8,128)(2,1)}, f32[8192,512]{1,0:T(8,128)}) fusion(f32[512]{0:T(512)S(1)} %copy-done.31, bf16[8192,1024]{1,0:T(8,128)(2,1)} %all-gather.9.cloned.1.call-done, bf16[1024,512]{1,0:T(8,128)(2,1)} %all-gather.11.cloned.1.call-done), kind=kOutput, calls=%fused_computation.68 | convolution fusion | flops 8866758656 | bytes 42993664 | tf_op jit(solution)/shard_map/dot_general | solution.py:145
  674.2 14.8 convolution_convert_fusion.1
  689.0 166.3 %reduce-scatter.11.cloned.1.call-done = bf16[1024,1024]{1,0:T(8,128)(2,1)} async-done(((bf16[8192,1024]{1,0:T(8,128)(2,1)}), bf16[1024,1024]{1,0:T(8,128)(2,1)}) %reduce-scatter.11.cloned.1.call-update) | async-done | bytes 2097168 | tf_op jit(solution)/shard_map/reduce_scatter | solution.py:148
  871.4 149.7 %all-gather.15.cloned.1.call-done = bf16[8192,1024]{1,0:T(8,128)(2,1)} async-done(((bf16[1024,1024]{1,0:T(8,128)(2,1)}), bf16[8192,1024]{1,0:T(8,128)(2,1)}) %all-gather.15.cloned.1.call-update) | async-done | bytes 16777232 | tf_op jit(solution)/shard_map/all_gather | solution.py:161
  1021.1 22.2 %fusion.107 = (f32[512]{0:T(512)}, bf16[8192,512]{1,0:T(8,128)(2,1)}) fusion(f32[8192,512]{1,0:T(8,128)} %get-tuple-element.248, f32[512]{0:T(512)S(1)} %copy-done.31, bf16[8192,1024]{1,0:T(8,128)(2,1)} %all-gather.15.cloned.1.call-done, bf16[512,1024]{1,0:T(8,128)(2,1)S(1)} %copy-done.30), kind=kOutput, calls=%fused_computation.157 | convolution fusion | flops 8640266240 | bytes 42995712 | tf_op jit(solution)/shard_map/dot_general | solution.py:166
  1043.3 18.7 fusion.87
  1062.1 323.6 %reduce-scatter.13.cloned.1.call-done = f32[1024,1024]{1,0:T(8,128)} async-done(((f32[8192,1024]{1,0:T(8,128)}), f32[1024,1024]{1,0:T(8,128)}) %reduce-scatter.13.cloned.1.call-update) | async-done | bytes 4194320 | tf_op jit(solution)/shard_map/reduce_scatter | solution.py:178
  1398.6 15.9 fusion.91
  1414.7 16.2 convolution_convert_fusion.3
  1430.9 117.4 %all-gather.17.cloned.1.call-done = bf16[8192,1024]{1,0:T(8,128)(2,1)} async-done(((bf16[1024,1024]{1,0:T(8,128)(2,1)}), bf16[8192,1024]{1,0:T(8,128)(2,1)}) %all-gather.17.cloned.1.call-update) | async-done | bytes 16777232 | tf_op jit(solution)/shard_map/all_gather | solution.py:189
  1548.3 8.3 convolution_convert_fusion.2
  1560.0 9.1 copy.56
  1569.1 160.9 %while.27 = (s32[]{:T(128)}, f32[8,1024,2,64]{1,3,2,0:T(8,128)}, bf16[8,1024,2,64]{1,3,2,0:T(8,128)(2,1)}, f32[8,1024,2,64]{1,3,2,0:T(8,128)}, bf16[8,1024,2,64]...) while((s32[]{:T(128)}, f32[8,1024,2,64]{1,3,2,0:T(8,128)}, ...), condition=%wide.region_17.18_spmd, body=%wide.region_15.17_spmd.sunk | while | flops 1374943232 | bytes 70591616 | solution.py:196
  1736.5 10.8 copy.74
  1747.3 8.2 reshape.198
  1762.8 7.9 reshape.200
  1770.7 7.3 copy.75
  1778.1 7.9 reshape.199
  1789.1 8.8 convolution_convert_fusion.4
  1802.6 13.0 fusion.97
  1815.7 15.7 reduce-scatter.17.cloned.1.call-done
  1831.4 14.5 bitcast_convert_fusion
  1847.0 41.2 %all-reduce = (f32[2,1024]{1,0:T(2,128)S(1)}, f32[1024]{0:T(1024)}, f32[1024]{0:T(1024)}, f32[1024]{0:T(1024)}, f32[4096]{0:T(1024)S(1)}, /*index=5*/f32[1024]{0:T(1024)}, f32[1024]{0:T(1024)}, f32[1024]{0:T(1024)}) all-reduce(f32[2,1024]{1,0:T(2,128)S(1)} %maximum_dynamic-update-sl, ...), channel_id=1, replica_groups=mesh['replica'=2,'shard'=2,'tensor'=8] {'replica','shard','tensor'}, use_global_device_ids=true, to_apply=%region_23.24 | all-reduce | flops 12288 | bytes 98304 | tf_op jit(solution)/shard_map/psum | solution.py:256
  1897.5 156.9 %reduce-scatter.15.cloned.1.call-done = bf16[1024,1024]{1,0:T(8,128)(2,1)} async-done(((bf16[8192,1024]{1,0:T(8,128)(2,1)}), bf16[1024,1024]{1,0:T(8,128)(2,1)}) %reduce-scatter.15.cloned.1.call-update) | async-done | bytes 2097168 | tf_op jit(solution)/shard_map/reduce_scatter | solution.py:214
  (277 shorter events, 359.6 us)
Async XLA Ops:
  8.0 156.2 %all-gather.7.cloned.1.call-start = ((), (), s32[]{:S(2)}) async-start(), calls=%async_computation.8 | async-start | bytes 18874368 | tf_op jit(solution)/shard_map/all_gather | solution.py:25
  8.7 462.5 %reduce-scatter.9.cloned.1.call-start = ((), (), s32[]{:S(2)}) async-start(), calls=%async_computation.9 | async-start | bytes 18874368 | tf_op jit(solution)/shard_map/reduce_scatter | solution.py:135
  18.3 278.0 %copy-start.12 = (bf16[128,1024]{1,0:T(8,128)(2,1)}, bf16[128,1024]{1,0:T(8,128)(2,1)S(1)}, u32[]{:S(2)}) copy-start(bf16[128,1024]{1,0:T(8,128)(2,1)S(1)} %all_gather.30) | copy-start | bytes 786436
  29.2 148.2 %copy-start.14 = (bf16[3,1024,128]{1,2,0:T(8,128)(2,1)}, bf16[3,1024,128]{1,2,0:T(8,128)(2,1)S(1)}, u32[]{:S(2)}) copy-start(bf16[3,1024,128]{1,2,0:T(8,128)(2,1)S(1)} %all_gather.28) | copy-start | bytes 2359300
  296.3 8.3 copy-start.5
  304.6 166.6 %copy-start = (bf16[1024,1024]{1,0:T(8,128)(2,1)S(1)}, bf16[1024,1024]{1,0:T(8,128)(2,1)}, u32[]{:S(2)}) copy-start(bf16[1024,1024]{1,0:T(8,128)(2,1)} %param.19) | copy-start | bytes 6291460
  304.7 166.6 %copy-start.16 = (f32[1024]{0:T(1024)S(1)}, f32[1024]{0:T(1024)}, u32[]{:S(2)}) copy-start(f32[1024]{0:T(1024)} %param.24) | copy-start | bytes 12292
  304.7 173.3 %all-gather.11.cloned.1.call-start = ((), (), s32[]{:S(2)}) async-start(), calls=%async_computation.11 | async-start | bytes 1572864 | tf_op jit(solution)/shard_map/all_gather | solution.py:19
  305.3 169.5 %copy-start.17 = (f32[1024]{0:T(1024)S(1)}, f32[1024]{0:T(1024)}, u32[]{:S(2)}) copy-start(f32[1024]{0:T(1024)} %param.25) | copy-start | bytes 12292
  305.3 169.5 %copy-start.21 = (f32[1024]{0:T(1024)S(1)}, f32[1024]{0:T(1024)}, u32[]{:S(2)}) copy-start(f32[1024]{0:T(1024)} %param.26) | copy-start | bytes 12292
  305.3 321.6 %all-gather.9.cloned.1.call-start = ((), (), s32[]{:S(2)}) async-start(), calls=%async_computation.10 | async-start | bytes 18874368 | tf_op jit(solution)/shard_map/all_gather | solution.py:29
  474.8 152.0 %copy-start.31 = (f32[512]{0:T(512)S(1)}, f32[512]{0:T(512)}, u32[]{:S(2)}) copy-start(f32[512]{0:T(512)} %param.28) | copy-start | bytes 6148
  477.3 196.9 %all-gather.13.cloned.1.call-start = ((), (), s32[]{:S(2)}) async-start(), calls=%async_computation.12 | async-start | bytes 1572864 | tf_op jit(solution)/shard_map/all_gather | solution.py:20
  477.9 377.5 %reduce-scatter.11.cloned.1.call-start = ((), (), s32[]{:S(2)}) async-start(), calls=%async_computation.13 | async-start | bytes 18874368 | tf_op jit(solution)/shard_map/reduce_scatter | solution.py:148
  689.0 166.4 %copy-start.27 = (f32[1024]{0:T(1024)S(1)}, f32[1024]{0:T(1024)}, u32[]{:S(2)}) copy-start(f32[1024]{0:T(1024)} %param.30) | copy-start | bytes 12292
  689.0 332.1 %all-gather.15.cloned.1.call-start = ((), (), s32[]{:S(2)}) async-start(), calls=%async_computation.14 | async-start | bytes 18874368 | tf_op jit(solution)/shard_map/all_gather | solution.py:161
  869.6 151.5 %copy-start.30 = (bf16[512,1024]{1,0:T(8,128)(2,1)S(1)}, bf16[512,1024]{1,0:T(8,128)(2,1)}, u32[]{:S(2)}) copy-start(bf16[512,1024]{1,0:T(8,128)(2,1)} %all-gather.13.cloned.1.call-done) | copy-start | bytes 3145732
  871.3 514.4 %reduce-scatter.13.cloned.1.call-start = ((), (), s32[]{:S(2)}) async-start(), calls=%async_computation.15 | async-start | bytes 37748736 | tf_op jit(solution)/shard_map/reduce_scatter | solution.py:178
  1021.1 22.3 %copy-start.29 = (bf16[1024,512]{1,0:T(8,128)(2,1)S(1)}, bf16[1024,512]{1,0:T(8,128)(2,1)}, u32[]{:S(2)}) copy-start(bf16[1024,512]{1,0:T(8,128)(2,1)} %all-gather.11.cloned.1.call-done) | copy-start | bytes 3145732
  1062.1 486.2 %all-gather.17.cloned.1.call-start = ((), (), s32[]{:S(2)}) async-start(), calls=%async_computation.16 | async-start | bytes 18874368 | tf_op jit(solution)/shard_map/all_gather | solution.py:189
  1385.7 6.6 copy-start.2
  1398.5 417.1 %reduce-scatter.21.cloned.1.call-start = ((), (), s32[]{:S(2)}) async-start(), calls=%async_computation.20 | async-start | bytes 1572864 | tf_op jit(solution)/shard_map/reduce_scatter | solution.py:230
  1414.6 133.7 %copy-start.13 = (bf16[128,1024]{1,0:T(8,128)(2,1)S(1)}, bf16[128,1024]{1,0:T(8,128)(2,1)}, u32[]{:S(2)}) copy-start(bf16[128,1024]{1,0:T(8,128)(2,1)} %copy-done.12) | copy-start | bytes 786436
  1414.6 401.0 %reduce-scatter.23.cloned.1.call-start = ((), (), s32[]{:S(2)}) async-start(), calls=%async_computation.21 | async-start | bytes 1572864 | tf_op jit(solution)/shard_map/reduce_scatter | solution.py:233
  1430.8 384.8 %reduce-scatter.19.cloned.1.call-start = ((), (), s32[]{:S(2)}) async-start(), calls=%async_computation.19 | async-start | bytes 393216 | tf_op jit(solution)/shard_map/reduce_scatter | solution.py:227
  1730.0 4.6 copy-start.10
  1762.8 7.9 copy-start.11
  1778.1 11.0 copy-start.6
  1797.9 33.5 %reduce-scatter.17.cloned.1.call-start = ((), (), s32[]{:S(2)}) async-start(), calls=%async_computation.18 | async-start | bytes 1179648 | tf_op jit(solution)/shard_map/reduce_scatter | solution.py:224
  1802.6 28.9 %copy-start.15 = (bf16[3,1024,128]{1,2,0:T(8,128)(2,1)S(1)}, bf16[3,1024,128]{1,2,0:T(8,128)(2,1)}, u32[]{:S(2)}) copy-start(bf16[3,1024,128]{1,2,0:T(8,128)(2,1)} %copy-done.14) | copy-start | bytes 2359300
  1815.6 73.9 %all-reduce.4.cloned.1.call-start = ((), (), s32[]{:S(2)}) async-start(), calls=%async_computation.22 | async-start | bytes 3145728 | tf_op jit(solution)/shard_map/psum | solution.py:238
  1831.4 223.0 %reduce-scatter.15.cloned.1.call-start = ((), (), s32[]{:S(2)}) async-start(), calls=%async_computation.17 | async-start | bytes 18874368 | tf_op jit(solution)/shard_map/reduce_scatter | solution.py:214
  (15 other events, 27.3 us)
Sparse Core Ops, SparseCore 0:
  10.4 153.7 all-gather.6
  304.8 166.3 reduce-scatter.8
  871.4 149.5 all-gather.14
  1398.7 149.6 all-gather.16
  1831.5 52.2 all-reduce.3
  1886.0 168.3 reduce-scatter.14
Sparse Core Ops, SparseCore 1:
  306.7 19.3 all-gather.10
  477.4 149.4 all-gather.8
  628.3 19.3 all-gather.12
  689.1 166.2 reduce-scatter.10
  1062.2 323.5 reduce-scatter.12
  1414.7 18.5 reduce-scatter.20
  1435.9 20.3 reduce-scatter.22
  1798.0 9.8 reduce-scatter.18
  1815.6 15.7 reduce-scatter.16
where the time goes:
time: 2080 us; the launch traced here: 2070 us
  waiting for transfers between devices  1380 us (66%)
  matrix products  381 us (18%)
  local copies, waits for them, and re-layouts  121 us (6%)
  other arithmetic  108 us (5%)
  blocking collectives  59.6 us (3%)
    reduce_scatter x1, waiting for transfers between devices, body(): lax.psum_scatter(lax.dot_general(row_block, w_up, CONTRACT_COLS, preferre...  324 us
    reduce_scatter x1, waiting for transfers between devices, body(): lax.psum_scatter(jnp.dot(row_block, w_down, preferred_element_type=jnp.fl...  166 us
    reduce_scatter x1, waiting for transfers between devices, body(): lax.psum_scatter(jnp.dot(row_block, w_out, preferred_element_type=jnp.flo...  166 us
    reduce_scatter x1, waiting for transfers between devices, body(): lax.psum_scatter(jnp.einsum('jtc,jdc->td', row_block, w_qkv, preferred_el...  157 us
    all_gather x1, waiting for transfers between devices, body(): rows_branch = lax.all_gather(branch_grad, 'tensor', axis=0, tiled=True)  150 us
    all_gather x1, waiting for transfers between devices, middle_rows(): return lax.all_gather(hidden_low, 'tensor', axis=0, tiled=True)  149 us
    all_gather x1, waiting for transfers between devices, input_rows(): return lax.all_gather(layer_input, 'tensor', axis=0, tiled=True)  135 us
    all_gather x1, waiting for transfers between devices, body(): rows_attn = lax.all_gather(attn_grad, 'tensor', axis=0, tiled=True)  117 us
  transfers between devices with their start and end apart: 15, of which 9 were waited for; matrix products, arithmetic and copies ran while one was open for 18% of the time, Pallas kernels for 0%

commit v1 on v0

--- a/solution.py
+++ b/solution.py
@@ -10,6 +10,18 @@
 NEG_FILL = -1e30
 CONTRACT_ROWS = (((0,), (0,)), ((), ()))
 CONTRACT_COLS = (((1,), (1,)), ((), ()))
+
+
+def gather_by_bits(array, axis, dim):
+    ways, here, lap = (lax.axis_size(axis), lax.axis_index(axis), array.shape[dim])
+    line, have = (array, 1)
+    while have < ways:
+        line = jnp.concatenate(
+            [line, lax.ppermute(line, axis, [(d, (d - have) % ways) for d in range(ways)])],
+            axis=dim,
+        )
+        have = 2 * have
+    return jnp.roll(line, here * lap, axis=dim)
 
 
 def layer_weights(qkv_weight, out_weight, up_weight, down_weight):
@@ -186,7 +198,7 @@
     )
     out_bias_part = jnp.sum(resid_one_grad, axis=0)
     attn_grad = resid_one_grad.astype(jnp.bfloat16)
-    rows_attn = lax.all_gather(attn_grad, "tensor", axis=0, tiled=True)
+    rows_attn = gather_by_bits(attn_grad, "tensor", 0)
     out_grad_part = lax.dot_general(
         mixed_rows, rows_attn, CONTRACT_ROWS, preferred_element_type=jnp.float32
     )

time: 2080 us -> 2440 us (1.17)
  waiting for transfers between devices: 1380 us -> 1710 us
  local copies, waits for them, and re-layouts: 121 us -> 146 us
    ppermute x0 -> x3, waiting for transfers between devices: none -> 440 us  [gather_by_bits(): lax.ppermute(line, axis, [(d, (d - have) % ways) for d in range(ways)])]
    all_gather x1 -> x0, waiting for transfers between devices: 117 us -> none  [body(): rows_attn = lax.all_gather(attn_grad, 'tensor', axis=0, tiled=True)]
  transfers between devices with their start and end apart: 15 -> 17, of which waited for: 9 -> 11; matrix products, arithmetic and copies ran while one was open for 18% -> 17% of each run, Pallas kernels for 0% -> 0%
where the time goes in v1:
time: 2440 us; the launch traced here: 2430 us
  waiting for transfers between devices  1710 us (70%)
  matrix products  381 us (16%)
  local copies, waits for them, and re-layouts  146 us (6%)
  other arithmetic  116 us (5%)
  blocking collectives  59.6 us (2%)
    ppermute x3, waiting for transfers between devices, gather_by_bits(): lax.ppermute(line, axis, [(d, (d - have) % ways) for d in range(ways)])  440 us
    reduce_scatter x1, waiting for transfers between devices, body(): lax.psum_scatter(lax.dot_general(row_block, w_up, CONTRACT_COLS, preferre...  324 us
    reduce_scatter x1, waiting for transfers between devices, body(): lax.psum_scatter(jnp.dot(row_block, w_down, preferred_element_type=jnp.fl...  166 us
    reduce_scatter x1, waiting for transfers between devices, body(): lax.psum_scatter(jnp.dot(row_block, w_out, preferred_element_type=jnp.flo...  166 us
    reduce_scatter x1, waiting for transfers between devices, body(): lax.psum_scatter(jnp.einsum('jtc,jdc->td', row_block, w_qkv, preferred_el...  157 us
    all_gather x1, waiting for transfers between devices, body(): rows_branch = lax.all_gather(branch_grad, 'tensor', axis=0, tiled=True)  150 us
    all_gather x1, waiting for transfers between devices, middle_rows(): return lax.all_gather(hidden_low, 'tensor', axis=0, tiled=True)  149 us
    all_gather x1, waiting for transfers between devices, input_rows(): return lax.all_gather(layer_input, 'tensor', axis=0, tiled=True)  135 us
  transfers between devices with their start and end apart: 17, of which 11 were waited for; matrix products, arithmetic and copies ran while one was open for 17% of the time, Pallas kernels for 0%

profile of v1, /device:TPU:0, one launch (start us, length us, event | category | flops | bytes accessed | tf_op | source)
XLA Modules:
  0.0 2429.1 jit_solution(14978242822464065466)
XLA Ops:
  18.3 10.9 all_gather.25
  29.3 135.0 %all-gather.6.cloned.1.call-done = bf16[8192,1024]{1,0:T(8,128)(2,1)} async-done(((bf16[1024,1024]{1,0:T(8,128)(2,1)}), bf16[8192,1024]{1,0:T(8,128)(2,1)}) %all-gather.6.cloned.1.call-update) | async-done | bytes 16777232 | tf_op jit(solution)/shard_map/all_gather | solution.py:37
  164.3 13.5 fusion.77
  201.0 90.2 %while.26 = (s32[]{:T(128)}, bf16[8,1024,2,64]{1,3,2,0:T(8,128)(2,1)}, f32[8,2,1024,1]{2,1,3,0:T(2,128)}, bf16[8,1024,2,64]{1,3,2,0:T(8,128)(2,1)}, s32[8,1024]{...) while((s32[]{:T(128)}, ...), condition=%wide.region_3.4_spmd, body=%wide.region_0.3_spmd.sunk | while | flops 563214336 | bytes 30488676 | solution.py:142
  296.2 8.5 convolution_convert_fusion
  305.4 165.8 %reduce-scatter.9.cloned.1.call-done = bf16[1024,1024]{1,0:T(8,128)(2,1)} async-done(((bf16[8192,1024]{1,0:T(8,128)(2,1)}), bf16[1024,1024]{1,0:T(8,128)(2,1)}) %reduce-scatter.9.cloned.1.call-update) | async-done | bytes 2097168 | tf_op jit(solution)/shard_map/reduce_scatter | solution.py:147
  479.6 148.9 %all-gather.8.cloned.1.call-done = bf16[8192,1024]{1,0:T(8,128)(2,1)} async-done(((bf16[1024,1024]{1,0:T(8,128)(2,1)}), bf16[8192,1024]{1,0:T(8,128)(2,1)}) %all-gather.8.cloned.1.call-update) | async-done | bytes 16777232 | tf_op jit(solution)/shard_map/all_gather | solution.py:41
  628.4 47.3 %fusion.56 = (bf16[8192,512]{1,0:T(8,128)(2,1)}, f32[8192,512]{1,0:T(8,128)}) fusion(f32[512]{0:T(512)S(1)} %copy-done.32, bf16[8192,1024]{1,0:T(8,128)(2,1)} %all-gather.8.cloned.1.call-done, bf16[1024,512]{1,0:T(8,128)(2,1)} %all-gather.10.cloned.1.call-done), kind=kOutput, calls=%fused_computation.68 | convolution fusion | flops 8866758656 | bytes 42993664 | tf_op jit(solution)/shard_map/dot_general | solution.py:157
  675.8 14.8 convolution_convert_fusion.1
  690.6 166.3 %reduce-scatter.11.cloned.1.call-done = bf16[1024,1024]{1,0:T(8,128)(2,1)} async-done(((bf16[8192,1024]{1,0:T(8,128)(2,1)}), bf16[1024,1024]{1,0:T(8,128)(2,1)}) %reduce-scatter.11.cloned.1.call-update) | async-done | bytes 2097168 | tf_op jit(solution)/shard_map/reduce_scatter | solution.py:160
  871.9 149.7 %all-gather.14.cloned.1.call-done = bf16[8192,1024]{1,0:T(8,128)(2,1)} async-done(((bf16[1024,1024]{1,0:T(8,128)(2,1)}), bf16[8192,1024]{1,0:T(8,128)(2,1)}) %all-gather.14.cloned.1.call-update) | async-done | bytes 16777232 | tf_op jit(solution)/shard_map/all_gather | solution.py:173
  1021.6 22.3 fusion.119
  1043.9 18.7 fusion.94
  1062.7 323.6 %reduce-scatter.13.cloned.1.call-done = f32[1024,1024]{1,0:T(8,128)} async-done(((f32[8192,1024]{1,0:T(8,128)}), f32[1024,1024]{1,0:T(8,128)}) %reduce-scatter.13.cloned.1.call-update) | async-done | bytes 4194320 | tf_op jit(solution)/shard_map/reduce_scatter | solution.py:190
  1399.7 23.6 collective-permute-done
  1425.5 91.1 %collective-permute-done.1 = bf16[2048,1024]{1,0:T(8,128)(2,1)S(1)} collective-permute-done((bf16[2048,1024]{1,0:T(8,128)(2,1)S(1)}, bf16[2048,1024]{1,0:T(8,128)(2,1)S(1)}, u32[]{:S(2)}, u32[]{:S(2)}) %collective-permute-start.1) | collective-permute-done | bytes 4194336 | tf_op jit(solution)/shard_map/ppermute | solution.py:20
  1522.2 15.6 fusion.98
  1537.9 15.7 convolution_convert_fusion.2
  1559.4 325.0 %collective-permute-done.2 = bf16[4096,1024]{1,0:T(8,128)(2,1)} collective-permute-done((bf16[4096,1024]{1,0:T(8,128)(2,1)}, bf16[4096,1024]{1,0:T(8,128)(2,1)}, u32[]{:S(2)}, u32[]{:S(2)}) %collective-permute-start.2) | collective-permute-done | bytes 8388640 | tf_op jit(solution)/shard_map/ppermute | solution.py:20
  1906.6 8.3 fusion.80
  1918.3 9.1 copy.56
  1927.4 160.8 %while.27 = (s32[]{:T(128)}, f32[8,1024,2,64]{1,3,2,0:T(8,128)}, bf16[8,1024,2,64]{1,3,2,0:T(8,128)(2,1)}, f32[8,1024,2,64]{1,3,2,0:T(8,128)}, bf16[8,1024,2,64]...) while((s32[]{:T(128)}, f32[8,1024,2,64]{1,3,2,0:T(8,128)}, ...), condition=%wide.region_17.18_spmd, body=%wide.region_15.17_spmd.sunk | while | flops 1374943232 | bytes 70591616 | solution.py:208
  2099.4 8.0 reshape.198
  2118.7 7.8 reshape.200
  2126.5 10.9 copy.75
  2137.4 7.8 reshape.199
  2145.2 8.8 fusion.107
  2161.8 13.0 fusion.104
  2174.9 17.5 reduce-scatter.17.cloned.1.call-done
  2192.5 14.6 bitcast_convert_fusion
  2208.2 41.3 %all-reduce = (f32[2,1024]{1,0:T(2,128)S(1)}, f32[1024]{0:T(1024)}, f32[1024]{0:T(1024)}, f32[1024]{0:T(1024)}, f32[4096]{0:T(1024)S(1)}, /*index=5*/f32[1024]{0:T(1024)}, f32[1024]{0:T(1024)}, f32[1024]{0:T(1024)}) all-reduce(f32[2,1024]{1,0:T(2,128)S(1)} %maximum_dynamic-update-sl, ...), channel_id=1, replica_groups=mesh['replica'=2,'shard'=2,'tensor'=8] {'replica','shard','tensor'}, use_global_device_ids=true, to_apply=%region_23.24 | all-reduce | flops 12288 | bytes 98304 | tf_op jit(solution)/shard_map/psum | solution.py:268
  2258.7 156.8 %reduce-scatter.15.cloned.1.call-done = bf16[1024,1024]{1,0:T(8,128)(2,1)} async-done(((bf16[8192,1024]{1,0:T(8,128)(2,1)}), bf16[1024,1024]{1,0:T(8,128)(2,1)}) %reduce-scatter.15.cloned.1.call-update) | async-done | bytes 2097168 | tf_op jit(solution)/shard_map/reduce_scatter | solution.py:226
  (291 shorter events, 412.2 us)
Async XLA Ops:
  8.0 156.2 %all-gather.6.cloned.1.call-start = ((), (), s32[]{:S(2)}) async-start(), calls=%async_computation.8 | async-start | bytes 18874368 | tf_op jit(solution)/shard_map/all_gather | solution.py:37
  8.7 462.5 %reduce-scatter.9.cloned.1.call-start = ((), (), s32[]{:S(2)}) async-start(), calls=%async_computation.9 | async-start | bytes 18874368 | tf_op jit(solution)/shard_map/reduce_scatter | solution.py:147
  18.3 277.8 %copy-start.13 = (bf16[128,1024]{1,0:T(8,128)(2,1)}, bf16[128,1024]{1,0:T(8,128)(2,1)S(1)}, u32[]{:S(2)}) copy-start(bf16[128,1024]{1,0:T(8,128)(2,1)S(1)} %all_gather.27) | copy-start | bytes 786436
  29.2 148.5 %copy-start.15 = (bf16[3,1024,128]{1,2,0:T(8,128)(2,1)}, bf16[3,1024,128]{1,2,0:T(8,128)(2,1)S(1)}, u32[]{:S(2)}) copy-start(bf16[3,1024,128]{1,2,0:T(8,128)(2,1)S(1)} %all_gather.25) | copy-start | bytes 2359300
  296.1 8.5 copy-start.8
  304.7 166.5 %copy-start = (bf16[1024,1024]{1,0:T(8,128)(2,1)S(1)}, bf16[1024,1024]{1,0:T(8,128)(2,1)}, u32[]{:S(2)}) copy-start(bf16[1024,1024]{1,0:T(8,128)(2,1)} %param.19) | copy-start | bytes 6291460
  304.7 166.5 %copy-start.17 = (f32[1024]{0:T(1024)S(1)}, f32[1024]{0:T(1024)}, u32[]{:S(2)}) copy-start(f32[1024]{0:T(1024)} %param.24) | copy-start | bytes 12292
  304.7 171.7 %copy-start.18 = (f32[1024]{0:T(1024)S(1)}, f32[1024]{0:T(1024)}, u32[]{:S(2)}) copy-start(f32[1024]{0:T(1024)} %param.25) | copy-start | bytes 12292
  304.7 171.7 %copy-start.22 = (f32[1024]{0:T(1024)S(1)}, f32[1024]{0:T(1024)}, u32[]{:S(2)}) copy-start(f32[1024]{0:T(1024)} %param.26) | copy-start | bytes 12292
  304.7 174.8 %all-gather.10.cloned.1.call-start = ((), (), s32[]{:S(2)}) async-start(), calls=%async_computation.11 | async-start | bytes 1572864 | tf_op jit(solution)/shard_map/all_gather | solution.py:31
  305.3 323.1 %all-gather.8.cloned.1.call-start = ((), (), s32[]{:S(2)}) async-start(), calls=%async_computation.10 | async-start | bytes 18874368 | tf_op jit(solution)/shard_map/all_gather | solution.py:41
  473.7 154.7 %copy-start.32 = (f32[512]{0:T(512)S(1)}, f32[512]{0:T(512)}, u32[]{:S(2)}) copy-start(f32[512]{0:T(512)} %param.28) | copy-start | bytes 6148
  478.9 196.9 %all-gather.12.cloned.1.call-start = ((), (), s32[]{:S(2)}) async-start(), calls=%async_computation.12 | async-start | bytes 1572864 | tf_op jit(solution)/shard_map/all_gather | solution.py:32
  479.5 377.4 %reduce-scatter.11.cloned.1.call-start = ((), (), s32[]{:S(2)}) async-start(), calls=%async_computation.13 | async-start | bytes 18874368 | tf_op jit(solution)/shard_map/reduce_scatter | solution.py:160
  690.6 166.3 %copy-start.28 = (f32[1024]{0:T(1024)S(1)}, f32[1024]{0:T(1024)}, u32[]{:S(2)}) copy-start(f32[1024]{0:T(1024)} %param.30) | copy-start | bytes 12292
  690.6 171.0 %copy-start.21 = (f32[1024]{0:T(1024)S(1)}, f32[1024]{0:T(1024)}, u32[]{:S(2)}) copy-start(f32[1024]{0:T(1024)} %param.31) | copy-start | bytes 12292
  690.6 331.0 %all-gather.14.cloned.1.call-start = ((), (), s32[]{:S(2)}) async-start(), calls=%async_computation.14 | async-start | bytes 18874368 | tf_op jit(solution)/shard_map/all_gather | solution.py:173
  868.1 153.5 %copy-start.31 = (bf16[512,1024]{1,0:T(8,128)(2,1)S(1)}, bf16[512,1024]{1,0:T(8,128)(2,1)}, u32[]{:S(2)}) copy-start(bf16[512,1024]{1,0:T(8,128)(2,1)} %all-gather.12.cloned.1.call-done) | copy-start | bytes 3145732
  871.8 514.5 %reduce-scatter.13.cloned.1.call-start = ((), (), s32[]{:S(2)}) async-start(), calls=%async_computation.15 | async-start | bytes 37748736 | tf_op jit(solution)/shard_map/reduce_scatter | solution.py:190
  1021.6 22.3 copy-start.30
  1062.6 1112.2 %reduce-scatter.21.cloned.1.call-start = ((), (), s32[]{:S(2)}) async-start(), calls=%async_computation.19 | async-start | bytes 1572864 | tf_op jit(solution)/shard_map/reduce_scatter | solution.py:242
  1399.6 122.6 %copy-start.7 = (bf16[1024,1024]{1,0:T(8,128)(2,1)}, bf16[1024,1024]{1,0:T(8,128)(2,1)S(1)}, u32[]{:S(2)}) copy-start(bf16[1024,1024]{1,0:T(8,128)(2,1)S(1)} %get-tuple-element.234) | copy-start | bytes 6291460
  1399.6 23.7 collective-permute-start
  1423.7 92.8 %collective-permute-start.1 = (bf16[2048,1024]{1,0:T(8,128)(2,1)S(1)}, bf16[2048,1024]{1,0:T(8,128)(2,1)S(1)}, u32[]{:S(2)}, u32[]{:S(2)}) collective-permute-start(bf16[2048,1024]{1,0:T(8,128)(2,1)S(1)} %pad_maximum_fusion.1), channel_id=1, source_target_pairs={{0,6},{1,7},{2,0},{3,1},{4,2},{5,3},{6,4},{7,5},{8,14},{9,15},{10,... | collective-permute-start | bytes 12582920 | tf_op jit(solution)/shard_map/ppermute | solution.py:20
  1521.1 363.4 %collective-permute-start.2 = (bf16[4096,1024]{1,0:T(8,128)(2,1)}, bf16[4096,1024]{1,0:T(8,128)(2,1)}, u32[]{:S(2)}, u32[]{:S(2)}) collective-permute-start(bf16[4096,1024]{1,0:T(8,128)(2,1)} %pad_maximum_fusion), channel_id=1, source_target_pairs={{0,4},{1,5},{2,6},{3,7},{4,0},{5,1},{6,2},{7,3},{8,12},{9,13},{10,... | collective-permute-start | bytes 25165832 | tf_op jit(solution)/shard_map/ppermute | solution.py:20
  1537.8 637.0 %reduce-scatter.23.cloned.1.call-start = ((), (), s32[]{:S(2)}) async-start(), calls=%async_computation.20 | async-start | bytes 1572864 | tf_op jit(solution)/shard_map/reduce_scatter | solution.py:245
  1553.6 621.3 %reduce-scatter.19.cloned.1.call-start = ((), (), s32[]{:S(2)}) async-start(), calls=%async_computation.18 | async-start | bytes 393216 | tf_op jit(solution)/shard_map/reduce_scatter | solution.py:239
  2126.5 18.7 copy-start.9
  2157.2 35.2 %reduce-scatter.17.cloned.1.call-start = ((), (), s32[]{:S(2)}) async-start(), calls=%async_computation.17 | async-start | bytes 1179648 | tf_op jit(solution)/shard_map/reduce_scatter | solution.py:236
  2161.7 30.8 %copy-start.16 = (bf16[3,1024,128]{1,2,0:T(8,128)(2,1)S(1)}, bf16[3,1024,128]{1,2,0:T(8,128)(2,1)}, u32[]{:S(2)}) copy-start(bf16[3,1024,128]{1,2,0:T(8,128)(2,1)} %copy-done.15) | copy-start | bytes 2359300
  2174.8 75.9 %all-reduce.4.cloned.1.call-start = ((), (), s32[]{:S(2)}) async-start(), calls=%async_computation.21 | async-start | bytes 3145728 | tf_op jit(solution)/shard_map/psum | solution.py:250
  2192.5 223.0 %reduce-scatter.15.cloned.1.call-start = ((), (), s32[]{:S(2)}) async-start(), calls=%async_computation.16 | async-start | bytes 18874368 | tf_op jit(solution)/shard_map/reduce_scatter | solution.py:226
  (18 other events, 56.1 us)
Sparse Core Ops, SparseCore 0:
  10.4 153.7 all-gather.5
  304.8 166.3 reduce-scatter.8
  871.9 149.5 all-gather.13
  2192.6 52.2 all-reduce.3
  2247.1 168.3 reduce-scatter.14
Sparse Core Ops, SparseCore 1:
  306.8 19.3 all-gather.9
  479.0 149.4 all-gather.7
  629.8 19.3 all-gather.11
  690.7 166.2 reduce-scatter.10
  1062.7 323.5 reduce-scatter.12
  1537.9 20.6 reduce-scatter.20
  1561.3 20.3 reduce-scatter.22
  2157.3 11.8 reduce-scatter.18
  2174.9 17.5 reduce-scatter.16
